TPU v7x, 128 devices: a whole 4x4x4 slice. The times are simulated.
128 devices in a mesh: row: 8 (over x, core), col: 16 (over z, y).
Axes of the slice: x: 4, y: 4, z: 4, core: 2. Of those that a mesh axis runs over, the one named last changes fastest.
Arguments:
- ham: bfloat16 [6144, 6144], P('row', 'col'), may hold values from -0.078125 to 0.078125
- deriv: bfloat16 [6144, 6144], P('row', 'col'), may hold values from -6 to 6
- band: int32 [48], replicated, may hold values from 1 to 24, as said below
- frag_of: int32 [48], replicated, may hold values from 0 to 31
Outputs:
- sign_iterate: bfloat16 [6144, 6144], P('row', 'col')
- energy_density: bfloat16 [6144, 6144], P('row', 'col')
- pulay_terms: float32 [32, 128], P('col')
Inputs may be any that keep to these rules, and one draw needn't show every extreme that they name: Some block row has band half-width exactly 24.
All inputs are finite; a program needn't handle non-finite values.
Results may differ from a plain program's by a relative error of at most 0.006.
Values may be sent and summed in bfloat16 or wider, within the bound.
A program may use at most 64 MiB of HBM per device.

v0:
```python
import jax
import jax.numpy as jnp
from jax import lax
from jax.sharding import PartitionSpec as P

BLK = 128
FRAG_DEV = 2


def column_panel_of(right_matrix):
    return lax.all_gather(right_matrix, "row", axis=0, tiled=True)


def folded_product(left_matrix, right_matrix):
    whole_panel = column_panel_of(right_matrix)
    return jnp.dot(
        lax.all_gather(left_matrix, "col", axis=1, tiled=True),
        whole_panel,
        preferred_element_type=jnp.float32,
    )


def body(ham, deriv, band, frag_of):
    rows_here = ham.shape[0]
    cols_here = ham.shape[1]
    block_rows = rows_here // BLK
    block_cols = cols_here // BLK
    row_index = lax.axis_index("row")
    col_index = lax.axis_index("col")
    row_blocks = row_index * block_rows + jnp.arange(block_rows, dtype=jnp.int32)
    col_blocks = col_index * block_cols + jnp.arange(block_cols, dtype=jnp.int32)
    row_band = lax.dynamic_slice_in_dim(band, row_index * block_rows, block_rows)
    col_band = lax.dynamic_slice_in_dim(band, col_index * block_cols, block_cols)
    widest = jnp.maximum(row_band[:, None], col_band[None, :])
    inside = jnp.abs(row_blocks[:, None] - col_blocks[None, :]) <= widest
    pattern = jnp.repeat(jnp.repeat(inside.astype(jnp.float32), BLK, axis=0), BLK, axis=1)
    global_rows = row_index * rows_here + jnp.arange(rows_here, dtype=jnp.int32)
    global_cols = col_index * cols_here + jnp.arange(cols_here, dtype=jnp.int32)
    identity = (global_rows[:, None] == global_cols[None, :]).astype(jnp.float32)
    start = (ham.astype(jnp.float32) * pattern).astype(jnp.bfloat16)

    def start_times(right_matrix):
        return folded_product(start, right_matrix)

    square = (start_times(start) * pattern).astype(jnp.bfloat16)
    cubic = start_times(square)
    sign_iterate = (pattern * (1.5 * start.astype(jnp.float32) - 0.5 * cubic)).astype(jnp.bfloat16)
    density = (0.5 * (identity - sign_iterate.astype(jnp.float32))).astype(jnp.bfloat16)
    weighted = (start_times(density) * pattern).astype(jnp.bfloat16)
    energy_density = (folded_product(density, weighted) * pattern).astype(jnp.bfloat16)
    column_terms = jnp.sum(energy_density.astype(jnp.float32) * deriv.astype(jnp.float32), axis=0)
    column_terms = column_terms.reshape(block_cols, BLK)
    local_frags = lax.dynamic_slice_in_dim(frag_of, col_index * block_cols, block_cols)
    fragment_count = FRAG_DEV * lax.axis_size("col")
    fragments = jnp.arange(fragment_count, dtype=jnp.int32)
    onehot = (local_frags[None, :] == fragments[:, None]).astype(jnp.float32)
    partial_value = jnp.dot(onehot, column_terms, precision=lax.Precision.HIGHEST)
    grand_total = lax.psum(partial_value, ("row", "col"))
    pulay_terms = lax.dynamic_slice_in_dim(grand_total, col_index * FRAG_DEV, FRAG_DEV, 0)
    return (sign_iterate, energy_density, pulay_terms)


def solution(mesh):
    placed = (P("row", "col"), P("row", "col"), P(), P())
    return jax.shard_map(
        body,
        mesh=mesh,
        in_specs=placed,
        out_specs=(P("row", "col"), P("row", "col"), P("col", None)),
        check_vma=False,
    )
```

profile of v0, /device:TPU:1, one launch (start us, length us, event | category | flops | bytes accessed | tf_op | source)
XLA Modules:
  0.0 432.5 jit_solution(7368020755092818838)
XLA Ops:
  7.2 0.0 all-gather.9.cloned.1.call-start
  7.2 0.7 dynamic_slice.13
  8.0 0.7 dynamic_slice.12
  8.7 0.1 fusion.9
  8.8 0.1 broadcast_bitcast_fusion
  8.9 0.1 broadcast_in_dim.5
  9.0 0.0 copy-start
  9.0 0.4 copy.8
  9.3 0.7 copy-done
  10.0 0.9 multiply_convert_fusion.1
  11.0 0.0 all-gather.9.cloned.1.call-update
  11.0 0.0 all-gather.7.cloned.1.call-start
  11.0 0.7 all-gather.7.cloned.1.call-update
  11.7 0.0 all-gather.11.cloned.1.call-start
  11.8 37.2 %all-gather.9.cloned.1.call-done = bf16[6144,384]{1,0:T(8,128)(2,1)} async-done(((bf16[768,384]{1,0:T(8,128)(2,1)}), bf16[6144,384]{1,0:T(8,128)(2,1)}) %all-gather.9.cloned.1.call-update) | async-done | bytes 4718608 | tf_op jit(solution)/shard_map/all_gather | solution.py:11
  48.9 83.6 %all-gather.7.cloned.1.call-done = bf16[768,6144]{1,0:T(8,128)(2,1)} async-done(((bf16[768,384]{1,0:T(8,128)(2,1)}), bf16[768,6144]{1,0:T(8,128)(2,1)}) %all-gather.7.cloned.1.call-update) | async-done | bytes 9437200 | tf_op jit(solution)/shard_map/all_gather | solution.py:17
  132.5 9.7 %fusion.3 = bf16[768,384]{0,1:T(8,128)(2,1)} fusion(f32[768,384]{0,1:T(8,128)S(1)} %bitcast.20, bf16[768,6144]{1,0:T(8,128)(2,1)} %all-gather.7.cloned.1.call-done, bf16[6144,384]{1,0:T(8,128)(2,1)} %all-gather.9.cloned.1.call-done), kind=kOutput, calls=%fused_computation.7 | convolution fusion | flops 3624468480 | bytes 15925248 | tf_op jit(solution)/shard_map/dot_general | solution.py:16
  142.2 0.0 all-gather.11.cloned.1.call-update
  142.3 0.0 all-gather.15.cloned.1.call-start
  142.3 35.3 %all-gather.11.cloned.1.call-done = bf16[6144,384]{0,1:T(8,128)(2,1)} async-done(((bf16[768,384]{0,1:T(8,128)(2,1)}), bf16[6144,384]{0,1:T(8,128)(2,1)}) %all-gather.11.cloned.1.call-update) | async-done | bytes 4718608 | tf_op jit(solution)/shard_map/all_gather | solution.py:11
  177.6 10.0 %multiply_convert_fusion = (bf16[768,384]{1,0:T(8,128)(2,1)}, bf16[768,384]{1,0:T(8,128)(2,1)}) fusion(s32[384]{0:T(512)S(1)} %iota_add_fusion.1, s32[768]{0:T(1024)S(1)} %iota_add_fusion, f32[768,384]{1,0:T(8,128)S(1)} %copy.8, bf16[768,6144]{1,0:T(8,128)(2,1)} %all-gather.7.cloned.1.call-done, bf16[6144,384]{0,1:T(8,128)(2,1)} %all-gather.11.cloned.1.call-done, ...), kind=kOutput, calls=%fused_computation.11 | convolution fusion | flops 3628302336 | bytes 17109504 | tf_op jit(solution)/shard_map/dot_general | solution.py:16
  187.6 0.0 all-gather.15.cloned.1.call-update
  187.6 0.0 all-gather.17.cloned.1.call-start
  187.7 34.3 %all-gather.15.cloned.1.call-done = bf16[6144,384]{1,0:T(8,128)(2,1)} async-done(((bf16[768,384]{1,0:T(8,128)(2,1)}), bf16[6144,384]{1,0:T(8,128)(2,1)}) %all-gather.15.cloned.1.call-update) | async-done | bytes 4718608 | tf_op jit(solution)/shard_map/all_gather | solution.py:11
  222.0 9.7 %fusion.4 = bf16[768,384]{0,1:T(8,128)(2,1)} fusion(f32[768,384]{0,1:T(8,128)S(1)} %bitcast.21, bf16[768,6144]{1,0:T(8,128)(2,1)} %all-gather.7.cloned.1.call-done, bf16[6144,384]{1,0:T(8,128)(2,1)} %all-gather.15.cloned.1.call-done), kind=kOutput, calls=%fused_computation.8 | convolution fusion | flops 3624468480 | bytes 15925248 | tf_op jit(solution)/shard_map/dot_general | solution.py:16
  231.7 0.0 copy-start.2
  231.7 0.0 copy-start.1
  231.7 0.0 all-gather.17.cloned.1.call-update
  231.7 0.2 all-gather.13.cloned.1.call-start
  231.9 0.3 all-gather.13.cloned.1.call-update
  232.3 0.0 copy-done.2
  232.3 0.1 dynamic_slice.14
  232.4 33.7 %all-gather.17.cloned.1.call-done = bf16[6144,384]{0,1:T(8,128)(2,1)} async-done(((bf16[768,384]{0,1:T(8,128)(2,1)}), bf16[6144,384]{0,1:T(8,128)(2,1)}) %all-gather.17.cloned.1.call-update) | async-done | bytes 4718608 | tf_op jit(solution)/shard_map/all_gather | solution.py:11
  266.1 83.4 %all-gather.13.cloned.1.call-done = bf16[768,6144]{1,0:T(8,128)(2,1)} async-done(((bf16[768,384]{1,0:T(8,128)(2,1)}), bf16[768,6144]{1,0:T(8,128)(2,1)}) %all-gather.13.cloned.1.call-update) | async-done | bytes 9437200 | tf_op jit(solution)/shard_map/all_gather | solution.py:17
  349.5 0.0 copy-done.1
  349.5 9.8 %multiply_reduce_fusion = (f32[384]{0:T(512)S(1)}, bf16[768,384]{1,0:T(8,128)(2,1)}) fusion(bf16[768,384]{1,0:T(8,128)(2,1)S(1)} %copy-done.1, f32[768,384]{1,0:T(8,128)S(1)} %copy.8, bf16[768,6144]{1,0:T(8,128)(2,1)} %all-gather.13.cloned.1.call-done, bf16[6144,384]{0,1:T(8,128)(2,1)} %all-gather.17.cloned.1.call-done), kind=kOutput, calls=%fused_computation.10 | convolution fusion | flops 3625647616 | bytes 16516608 | tf_op jit(solution)/shard_map/dot_general | solution.py:16
  359.3 0.1 fusion.6
  359.4 65.7 %psum.7 = f32[32,128]{1,0:T(8,128)S(1)} all-reduce(f32[32,128]{1,0:T(8,128)S(1)} %fusion.6), channel_id=1, replica_groups=mesh['row'=8,'col'=16] {'row','col'}, use_global_device_ids=true, to_apply=%region_1.0 | all-reduce | flops 4096 | bytes 32768 | tf_op jit(solution)/shard_map/psum | solution.py:58
  425.1 0.6 constant_dynamic-slice_fusion
  (5 shorter events, 0.0 us)
Async XLA Ops:
  7.2 41.8 %all-gather.9.cloned.1.call-start = ((), (), s32[]{:S(2)}) async-start(), calls=%async_computation.1 | async-start | bytes 5308416 | tf_op jit(solution)/shard_map/all_gather | solution.py:11
  9.0 1.1 copy-start
  11.0 121.6 %all-gather.7.cloned.1.call-start = ((), (), s32[]{:S(2)}) async-start(), calls=%async_computation | async-start | bytes 10027008 | tf_op jit(solution)/shard_map/all_gather | solution.py:17
  11.7 165.9 %all-gather.11.cloned.1.call-start = ((), (), s32[]{:S(2)}) async-start(), calls=%async_computation.2 | async-start | bytes 5308416 | tf_op jit(solution)/shard_map/all_gather | solution.py:11
  142.3 79.7 %all-gather.15.cloned.1.call-start = ((), (), s32[]{:S(2)}) async-start(), calls=%async_computation.4 | async-start | bytes 5308416 | tf_op jit(solution)/shard_map/all_gather | solution.py:11
  187.6 78.5 %all-gather.17.cloned.1.call-start = ((), (), s32[]{:S(2)}) async-start(), calls=%async_computation.5 | async-start | bytes 5308416 | tf_op jit(solution)/shard_map/all_gather | solution.py:11
  231.7 0.7 copy-start.2
  231.7 117.8 %copy-start.1 = (bf16[768,384]{1,0:T(8,128)(2,1)S(1)}, bf16[768,384]{1,0:T(8,128)(2,1)}, u32[]{:S(2)}) copy-start(bf16[768,384]{1,0:T(8,128)(2,1)} %param.5) | copy-start | bytes 1769476
  231.7 117.8 %all-gather.13.cloned.1.call-start = ((), (), s32[]{:S(2)}) async-start(), calls=%async_computation.3 | async-start | bytes 10027008 | tf_op jit(solution)/shard_map/all_gather | solution.py:17
Sparse Core Ops, SparseCore 0:
  11.1 37.7 all-gather.8
  51.6 80.8 all-gather.6
  142.4 35.1 all-gather.10
  187.7 34.2 all-gather.14
  231.8 34.2 all-gather.16
  268.6 80.8 all-gather.12
where the time goes:
time: 433 us
  waiting for transfers between devices  309 us (71%)
  blocking collectives  65.7 us (15%)
  matrix products  39.3 us (9%)
  between operations  14.2 us (3%)
    all_gather x2, waiting for transfers between devices, folded_product(): lax.all_gather(left_matrix, 'col', axis=1, tiled=True)  167 us
    all_gather x4, waiting for transfers between devices, column_panel_of(): return lax.all_gather(right_matrix, 'row', axis=0, tiled=True)  140 us
    psum x1, blocking collectives, body(): grand_total = lax.psum(partial_value, ('row', 'col'))  65.7 us
    dot_general x4, matrix products, folded_product(): jnp.dot(lax.all_gather(left_matrix, 'col', axis=1, tiled=True), whole_pan...  39.1 us
  transfers between devices with their start and end apart: 6, of which 6 were waited for; matrix products, arithmetic and copies ran while one was open for 0% of the time, Pallas kernels for 0%

commit v1 on v0

--- a/solution.py
+++ b/solution.py
@@ -14,7 +14,9 @@
 def folded_product(left_matrix, right_matrix):
     whole_panel = column_panel_of(right_matrix)
     return jnp.dot(
-        lax.all_gather(left_matrix, "col", axis=1, tiled=True),
+        jnp.concatenate(
+            lax.all_to_all(jnp.stack([left_matrix] * lax.axis_size("col")), "col", 0, 0), axis=1
+        ),
         whole_panel,
         preferred_element_type=jnp.float32,
     )

time: 433 us -> 452 us (1.044)
  starting transfers between devices: 0.42 us -> 15.7 us
  local copies, waits for them, and re-layouts: 3.37 us -> 14.1 us
    all_to_all x0 -> x2, waiting for transfers between devices: none -> 209 us  [folded_product(): lax.all_to_all(jnp.stack([left_matrix] * lax.axis_size('col')), 'col', 0, 0)]
    all_gather x2 -> x0, waiting for transfers between devices: 167 us -> none  [folded_product(): lax.all_gather(left_matrix, 'col', axis=1, tiled=True)]
    all_gather x4, waiting for transfers between devices: 140 us -> 95.7 us  [column_panel_of(): return lax.all_gather(right_matrix, 'row', axis=0, tiled=True)]
    all_to_all x0 -> x2, starting transfers between devices: none -> 15.4 us  [folded_product(): lax.all_to_all(jnp.stack([left_matrix] * lax.axis_size('col')), 'col', 0, 0)]
    another operation x0 -> x2, local copies, waits for them, and re-layouts: none -> 9.2 us  [folded_product(): jnp.stack([left_matrix] * lax.axis_size('col'))]
  transfers between devices with their start and end apart: 6 -> 6, of which waited for: 6 -> 5; matrix products, arithmetic and copies ran while one was open for 0% -> 3% of each run, Pallas kernels for 0% -> 0%
where the time goes in v1:
time: 452 us
  waiting for transfers between devices  305 us (67%)
  blocking collectives  63.2 us (14%)
  matrix products  39.5 us (9%)
  starting transfers between devices  15.7 us (3%)
  local copies, waits for them, and re-layouts  14.1 us (3%)
  between operations  13.9 us (3%)
    all_to_all x2, waiting for transfers between devices, folded_product(): lax.all_to_all(jnp.stack([left_matrix] * lax.axis_size('col')), 'col', 0, 0)  209 us
    all_gather x4, waiting for transfers between devices, column_panel_of(): return lax.all_gather(right_matrix, 'row', axis=0, tiled=True)  95.7 us
    psum x1, blocking collectives, body(): grand_total = lax.psum(partial_value, ('row', 'col'))  63.2 us
    dot_general x4, matrix products, folded_product(): jnp.dot(jnp.concatenate(lax.all_to_all(jnp.stack([left_matrix] * lax.axis...  39.4 us
    all_to_all x2, starting transfers between devices, folded_product(): lax.all_to_all(jnp.stack([left_matrix] * lax.axis_size('col')), 'col', 0, 0)  15.4 us
    another operation x2, local copies, waits for them, and re-layouts, folded_product(): jnp.stack([left_matrix] * lax.axis_size('col'))  9.2 us
  transfers between devices with their start and end apart: 6, of which 5 were waited for; matrix products, arithmetic and copies ran while one was open for 3% of the time, Pallas kernels for 0%

profile of v1, /device:TPU:1, one launch (start us, length us, event | category | flops | bytes accessed | tf_op | source)
XLA Modules:
  0.0 451.7 jit_solution(11445016482214334087)
XLA Ops:
  7.2 0.7 dynamic_slice.13
  7.9 0.7 dynamic_slice.12
  8.7 0.1 fusion.9
  8.7 0.1 broadcast_bitcast_fusion
  8.8 0.1 broadcast_in_dim.5
  8.9 0.0 copy-start.1
  8.9 0.4 copy.9
  9.3 0.7 copy-done.1
  10.0 0.1 multiply_convert_fusion.1
  10.1 0.0 copy-start
  10.1 0.3 copy.8
  10.4 4.6 %stack.4 = bf16[16,768,384]{1,2,0:T(8,128)(2,1)} broadcast(bf16[768,384]{0,1:T(8,128)(2,1)S(1)} %copy.8), dimensions={1,2} | broadcast | bytes 10027008 | tf_op jit(solution)/shard_map/stack | solution.py:18
  14.9 0.0 copy-done
  14.9 8.6 %all-to-all-start = ((bf16[16,768,384]{1,2,0:T(8,128)(2,1)}), bf16[16,768,384]{1,2,0:T(8,128)(2,1)}, u32[]{:S(2)}, u32[]{:S(2)}) async-start(bf16[16,768,384]{1,2,0:T(8,128)(2,1)} %stack.4), calls=%async_computation | async-start | bytes 18874368 | tf_op jit(solution)/shard_map/all_to_all | solution.py:18
  23.6 0.0 all-gather.5.cloned.1.call-start
  23.6 0.7 all-gather.5.cloned.1.call-update
  24.3 0.0 all-gather.7.cloned.1.call-start
  24.4 38.7 %all-gather.5.cloned.1.call-done = bf16[6144,384]{1,0:T(8,128)(2,1)} async-done(((bf16[768,384]{1,0:T(8,128)(2,1)}), bf16[6144,384]{1,0:T(8,128)(2,1)}) %all-gather.5.cloned.1.call-update) | async-done | bytes 4718608 | tf_op jit(solution)/shard_map/all_gather | solution.py:11
  63.1 99.4 %all-to-all-done = bf16[16,768,384]{1,2,0:T(8,128)(2,1)} async-done(((bf16[16,768,384]{1,2,0:T(8,128)(2,1)}), bf16[16,768,384]{1,2,0:T(8,128)(2,1)}, u32[]{:S(2)}, u32[]{:S(2)}) %all-to-all-start) | async-done | bytes 9437216 | tf_op jit(solution)/shard_map/all_to_all | solution.py:18
  162.5 0.0 copy-start.2
  162.5 9.8 %fusion = bf16[768,384]{0,1:T(8,128)(2,1)} fusion(f32[768,384]{0,1:T(8,128)S(1)} %bitcast.26, bf16[768,6144]{0,1:T(8,128)(2,1)} %bitcast.2, bf16[6144,384]{1,0:T(8,128)(2,1)} %all-gather.5.cloned.1.call-done), kind=kOutput, calls=%fused_computation.4 | convolution fusion | flops 3624468480 | bytes 15925248 | tf_op jit(solution)/shard_map/dot_general | solution.py:16
  172.3 0.0 all-gather.7.cloned.1.call-update
  172.4 0.0 all-gather.9.cloned.1.call-start
  172.4 35.5 %all-gather.7.cloned.1.call-done = bf16[6144,384]{0,1:T(8,128)(2,1)} async-done(((bf16[768,384]{0,1:T(8,128)(2,1)}), bf16[6144,384]{0,1:T(8,128)(2,1)}) %all-gather.7.cloned.1.call-update) | async-done | bytes 4718608 | tf_op jit(solution)/shard_map/all_gather | solution.py:11
  208.0 0.0 copy-done.2
  208.0 10.1 %multiply_convert_fusion = (bf16[768,384]{1,0:T(8,128)(2,1)}, bf16[768,384]{1,0:T(8,128)(2,1)}) fusion(s32[384]{0:T(512)S(1)} %iota_add_fusion.1, s32[768]{0:T(1024)S(1)} %iota_add_fusion, f32[768,384]{1,0:T(8,128)S(1)} %copy.9, bf16[768,6144]{0,1:T(8,128)(2,1)} %bitcast.2, bf16[6144,384]{0,1:T(8,128)(2,1)} %all-gather.7.cloned.1.call-done, ...), kind=kOutput, calls=%fused_computation.11 | convolution fusion | flops 3628302336 | bytes 17109504 | tf_op jit(solution)/shard_map/dot_general | solution.py:16
  218.1 0.0 all-gather.9.cloned.1.call-update
  218.1 1.3 copy.10
  219.4 4.6 %stack.5 = bf16[16,768,384]{1,2,0:T(8,128)(2,1)} broadcast(bf16[768,384]{0,1:T(8,128)(2,1)S(1)} %copy.10), dimensions={1,2} | broadcast | bytes 10027008 | tf_op jit(solution)/shard_map/stack | solution.py:18
  224.0 6.7 %all-to-all-start.1 = ((bf16[16,768,384]{1,2,0:T(8,128)(2,1)}), bf16[16,768,384]{1,2,0:T(8,128)(2,1)}, u32[]{:S(2)}, u32[]{:S(2)}) async-start(bf16[16,768,384]{1,2,0:T(8,128)(2,1)} %stack.5), calls=%async_computation.1 | async-start | bytes 18874368 | tf_op jit(solution)/shard_map/all_to_all | solution.py:18
  230.8 0.0 copy-start.4
  230.8 0.0 copy-start.3
  230.8 0.2 all-gather.11.cloned.1.call-start
  231.0 21.4 %all-gather.9.cloned.1.call-done = bf16[6144,384]{1,0:T(8,128)(2,1)} async-done(((bf16[768,384]{1,0:T(8,128)(2,1)}), bf16[6144,384]{1,0:T(8,128)(2,1)}) %all-gather.9.cloned.1.call-update) | async-done | bytes 4718608 | tf_op jit(solution)/shard_map/all_gather | solution.py:11
  252.5 9.7 %fusion.1 = bf16[768,384]{0,1:T(8,128)(2,1)} fusion(f32[768,384]{0,1:T(8,128)S(1)} %bitcast.27, bf16[768,6144]{0,1:T(8,128)(2,1)} %bitcast.2, bf16[6144,384]{1,0:T(8,128)(2,1)} %all-gather.9.cloned.1.call-done), kind=kOutput, calls=%fused_computation.5 | convolution fusion | flops 3624468480 | bytes 15925248 | tf_op jit(solution)/shard_map/dot_general | solution.py:16
  262.2 0.0 all-gather.11.cloned.1.call-update
  262.2 0.0 copy-done.4
  262.2 0.1 dynamic_slice.14
  262.3 109.3 %all-to-all-done.1 = bf16[16,768,384]{1,2,0:T(8,128)(2,1)} async-done(((bf16[16,768,384]{1,2,0:T(8,128)(2,1)}), bf16[16,768,384]{1,2,0:T(8,128)(2,1)}, u32[]{:S(2)}, u32[]{:S(2)}) %all-to-all-start.1) | async-done | bytes 9437216 | tf_op jit(solution)/shard_map/all_to_all | solution.py:18
  371.5 0.0 all-gather.11.cloned.1.call-done
  371.5 0.0 copy-done.3
  371.5 9.8 %multiply_reduce_fusion = (f32[384]{0:T(512)S(1)}, bf16[768,384]{1,0:T(8,128)(2,1)}) fusion(bf16[768,384]{1,0:T(8,128)(2,1)S(1)} %copy-done.3, f32[768,384]{1,0:T(8,128)S(1)} %copy.9, bf16[768,6144]{0,1:T(8,128)(2,1)} %bitcast.5, bf16[6144,384]{0,1:T(8,128)(2,1)} %all-gather.11.cloned.1.call-done), kind=kOutput, calls=%fused_computation.10 | convolution fusion | flops 3625647616 | bytes 16516608 | tf_op jit(solution)/shard_map/dot_general | solution.py:16
  381.3 0.1 fusion.6
  381.5 63.2 %psum.7 = f32[32,128]{1,0:T(8,128)S(1)} all-reduce(f32[32,128]{1,0:T(8,128)S(1)} %fusion.6), channel_id=1, replica_groups=mesh['row'=8,'col'=16] {'row','col'}, use_global_device_ids=true, to_apply=%region_1.0 | all-reduce | flops 4096 | bytes 32768 | tf_op jit(solution)/shard_map/psum | solution.py:60
  444.6 0.6 constant_dynamic-slice_fusion
  (5 shorter events, 0.0 us)
Async XLA Ops:
  8.9 1.1 copy-start.1
  10.1 4.8 %copy-start = (bf16[768,384]{1,0:T(8,128)(2,1)}, bf16[768,384]{1,0:T(8,128)(2,1)S(1)}, u32[]{:S(2)}) copy-start(bf16[768,384]{1,0:T(8,128)(2,1)S(1)} %multiply_convert_fusion.1) | copy-start | bytes 1769476
  14.9 147.6 %all-to-all-start = ((bf16[16,768,384]{1,2,0:T(8,128)(2,1)}), bf16[16,768,384]{1,2,0:T(8,128)(2,1)}, u32[]{:S(2)}, u32[]{:S(2)}) async-start(bf16[16,768,384]{1,2,0:T(8,128)(2,1)} %stack.4), calls=%async_computation | async-start | bytes 18874368 | tf_op jit(solution)/shard_map/all_to_all | solution.py:18
  23.6 39.5 %all-gather.5.cloned.1.call-start = ((), (), s32[]{:S(2)}) async-start(), calls=%async_computation.2 | async-start | bytes 5308416 | tf_op jit(solution)/shard_map/all_gather | solution.py:11
  24.3 183.7 %all-gather.7.cloned.1.call-start = ((), (), s32[]{:S(2)}) async-start(), calls=%async_computation.3 | async-start | bytes 5308416 | tf_op jit(solution)/shard_map/all_gather | solution.py:11
  162.5 45.5 %copy-start.2 = (bf16[768,384]{1,0:T(8,128)(2,1)S(1)}, bf16[768,384]{1,0:T(8,128)(2,1)}, u32[]{:S(2)}) copy-start(bf16[768,384]{1,0:T(8,128)(2,1)} %param.4) | copy-start | bytes 1769476
  172.4 80.1 %all-gather.9.cloned.1.call-start = ((), (), s32[]{:S(2)}) async-start(), calls=%async_computation.4 | async-start | bytes 5308416 | tf_op jit(solution)/shard_map/all_gather | solution.py:11
  224.0 147.5 %all-to-all-start.1 = ((bf16[16,768,384]{1,2,0:T(8,128)(2,1)}), bf16[16,768,384]{1,2,0:T(8,128)(2,1)}, u32[]{:S(2)}, u32[]{:S(2)}) async-start(bf16[16,768,384]{1,2,0:T(8,128)(2,1)} %stack.5), calls=%async_computation.1 | async-start | bytes 18874368 | tf_op jit(solution)/shard_map/all_to_all | solution.py:18
  230.8 31.4 %copy-start.4 = (s32[48]{0:T(128)S(1)}, s32[48]{0:T(128)}, u32[]{:S(2)}) copy-start(s32[48]{0:T(128)} %param.7) | copy-start | bytes 580
  230.8 140.7 %copy-start.3 = (bf16[768,384]{1,0:T(8,128)(2,1)S(1)}, bf16[768,384]{1,0:T(8,128)(2,1)}, u32[]{:S(2)}) copy-start(bf16[768,384]{1,0:T(8,128)(2,1)} %param.5) | copy-start | bytes 1769476
  230.8 140.7 %all-gather.11.cloned.1.call-start = ((), (), s32[]{:S(2)}) async-start(), calls=%async_computation.5 | async-start | bytes 5308416 | tf_op jit(solution)/shard_map/all_gather | solution.py:11
Sparse Core Ops, SparseCore 0:
  26.7 36.3 all-gather.4
  172.5 35.4 all-gather.6
  218.2 34.1 all-gather.8
  262.3 34.2 all-gather.10
